TPU v7x, 256 devices: a whole 4x4x8 slice. The times are simulated.
256 devices in a mesh: rows: 32 (over z_lo, y, x), cols: 8 (over z_hi, core).
Axes of the slice: x: 4, y: 4, z: 8 (z_hi: 4, z_lo: 2; z = z_hi * 2 + z_lo), core: 2. Of those that a mesh axis runs over, the one named last changes fastest.
Arguments:
- canvas: bfloat16 [256, 1024, 256], P('rows', 'cols'), may hold values from -16 to 16
- conv_weight: bfloat16 [3, 3, 256, 512], replicated, may hold values from -0.125 to 0.125
- conv_bias: bfloat16 [512], replicated, may hold values from -3 to 3
- target_gram: float32 [512, 512], P(('rows', 'cols')), may hold values from -6 to 6
Outputs:
- gram: float32 [512, 512], P(('rows', 'cols'))
- grad_canvas: bfloat16 [256, 1024, 256], P('rows', 'cols')
All inputs are finite; a program needn't handle non-finite values.
Results may differ from a plain program's by a relative error of at most 0.009.
Values may be sent and summed in bfloat16 or wider, within the bound.
A program may use at most 64 MiB of HBM per device.

v0:
```python
import math
import jax
import jax.numpy as jnp
from jax import lax
from jax.sharding import PartitionSpec as P

gelu_scale = math.sqrt(2.0 / math.pi)


def padded_2(block, sides, width):
    for axis, dim in sides:
        count = lax.axis_size(axis)
        forward = [(i, i + 1) for i in range(count - 1)]
        backward = [(target, source) for source, target in forward]
        low = lax.ppermute(
            lax.slice_in_dim(block, block.shape[dim] - width, None, axis=dim), axis, forward
        )
        high = lax.ppermute(lax.slice_in_dim(block, 0, width, axis=dim), axis, backward)
        block = jnp.concatenate([low, block, high], axis=dim)
    return block


def gelu_grad(value):
    tangent = jnp.tanh(gelu_scale * (value + 0.044715 * value * value * value))
    return 0.5 * (1.0 + tangent) + 0.5 * value * (1.0 - tangent * tangent) * gelu_scale * (
        1.0 + 3.0 * 0.044715 * value * value
    )


def patches(padded, tile_rows, tile_cols):
    pieces = [
        padded[row_off : row_off + tile_rows, col_off : col_off + tile_cols, :]
        for row_off in range(3)
        for col_off in range(3)
    ]
    return jnp.concatenate(pieces, axis=2).reshape(tile_rows * tile_cols, -1)


def on_device(canvas, conv_weight, conv_bias, target_gram):
    tile_rows, tile_cols, in_width = canvas.shape
    out_width = conv_weight.shape[3]
    pixel_total = tile_rows * tile_cols * lax.axis_size("rows") * lax.axis_size("cols")
    padded = padded_2(canvas, (("rows", 0), ("cols", 1)), 1)
    kernel = conv_weight.reshape(9 * in_width, out_width)
    preact = jnp.dot(
        patches(padded, tile_rows, tile_cols), kernel, preferred_element_type=jnp.float32
    ) + conv_bias.astype(jnp.float32)
    features = jax.nn.gelu(preact, approximate=True).astype(jnp.bfloat16)
    gram_own = (
        lax.psum_scatter(
            lax.dot_general(
                features, features, (((0,), (0,)), ((), ())), preferred_element_type=jnp.float32
            ),
            ("rows", "cols"),
            scatter_dimension=0,
            tiled=True,
        )
        / pixel_total
    )
    error_own = gram_own - target_gram
    error_full = lax.all_gather(error_own, ("rows", "cols"), axis=0, tiled=True)
    symmetric = (error_full + error_full.T).astype(jnp.bfloat16)
    upstream = jnp.dot(features, symmetric, preferred_element_type=jnp.float32) / math.sqrt(
        out_width
    )
    grad_pre = (
        (upstream * gelu_grad(preact)).astype(jnp.bfloat16).reshape(tile_rows, tile_cols, out_width)
    )
    grad_padded = padded_2(grad_pre, (("rows", 0), ("cols", 1)), 1)
    flipped = conv_weight[::-1, ::-1].transpose(0, 1, 3, 2).reshape(9 * out_width, in_width)
    grad_canvas = jnp.dot(
        patches(grad_padded, tile_rows, tile_cols), flipped, preferred_element_type=jnp.float32
    )
    return (gram_own, grad_canvas.astype(jnp.bfloat16).reshape(tile_rows, tile_cols, in_width))


def solution(mesh):
    return jax.shard_map(
        on_device,
        mesh=mesh,
        in_specs=(P("rows", "cols", None), P(), P(), P(("rows", "cols"), None)),
        out_specs=(P(("rows", "cols"), None), P("rows", "cols", None)),
        check_vma=False,
    )
```

profile of v0, /device:TPU:33, one launch (start us, length us, event | category | flops | bytes accessed | tf_op | source)
XLA Modules:
  0.0 724.9 jit_solution(6664298643092920723)
XLA Ops:
  8.2 3.1 collective-permute-start
  11.3 6.4 collective-permute-start.1
  19.0 6.6 collective-permute-start.2
  26.3 1.9 collective-permute-start.3
  28.4 3.8 collective-permute-done.3
  33.0 1.2 copy-done.1
  34.2 2.6 fusion.44
  36.8 1.3 copy-done.4
  38.1 2.8 fusion.30
  40.9 255.6 %all-reduce.3.cloned.1.call-done = f32[512,512]{1,0:T(8,128)} async-done(((f32[512,512]{1,0:T(8,128)}), f32[512,512]{1,0:T(8,128)}) %all-reduce.3.cloned.1.call-update) | async-done | bytes 1048592
  296.5 1.3 subtract_bitcast_fusion
  297.8 379.7 %all-gather.3.cloned.1.call-done = f32[256,2,512]{2,1,0:T(2,128)} async-done(((f32[1,2,512]{2,1,0:T(2,128)}), f32[256,2,512]{2,1,0:T(2,128)}) %all-gather.3.cloned.1.call-update) | async-done | bytes 1048592 | tf_op jit(solution)/shard_map/all_gather | solution.py:61
  677.5 1.9 reshape.39
  679.8 4.5 fusion.14
  685.0 5.2 collective-permute-start.5
  690.3 1.9 collective-permute-start.4
  692.2 2.8 copy.10
  695.0 1.6 rev.3
  696.6 4.5 collective-permute-done.4
  701.9 3.3 collective-permute-start.7
  705.3 3.6 collective-permute-start.6
  710.0 1.6 pad_maximum_fusion
  713.1 1.5 copy-done.2
  714.6 3.4 convolution_convert_fusion
  (46 shorter events, 8.3 us)
Async XLA Ops:
  7.2 21.2 %copy-start = (bf16[8,128,256]{2,1,0:T(8,128)(2,1)S(1)}, bf16[8,128,256]{2,1,0:T(8,128)(2,1)}, u32[]{:S(2)}) copy-start(bf16[8,128,256]{2,1,0:T(8,128)(2,1)} %param.4) | copy-start | bytes 1572868
  7.2 289.3 %all-reduce.3.cloned.1.call-start = ((), (), s32[]{:S(2)}) async-start(), calls=%async_computation.1 | async-start | bytes 2097152
  8.2 9.5 %collective-permute-start = (bf16[1,128,256]{2,1,0:T(8,128)(2,1)S(1)}, bf16[1,128,256]{2,1,0:T(8,128)(2,1)S(1)}, u32[]{:S(2)}, u32[]{:S(2)}) collective-permute-start(bf16[1,128,256]{2,1,0:T(8,128)(2,1)S(1)} %get-tuple-element.21), channel_id=1, source_target_pairs={{0,8},{8,16},{16,24},{24,32},{32,40},{40,48},{48,56},{56,64},{64,7... | collective-permute-start | bytes 196616 | tf_op jit(solution)/shard_map/ppermute | solution.py:15
  11.3 7.7 %collective-permute-start.1 = (bf16[1,128,256]{2,1,0:T(8,128)(2,1)S(1)}, bf16[1,128,256]{2,1,0:T(8,128)(2,1)S(1)}, u32[]{:S(2)}, u32[]{:S(2)}) collective-permute-start(bf16[1,128,256]{2,1,0:T(8,128)(2,1)S(1)} %get-tuple-element.20), channel_id=1, source_target_pairs={{8,0},{16,8},{24,16},{32,24},{40,32},{48,40},{56,48},{64,56},{72,6... | collective-permute-start | bytes 196616 | tf_op jit(solution)/shard_map/ppermute | solution.py:18
  19.0 9.2 %collective-permute-start.2 = (bf16[10,1,256]{2,1,0:T(2,128)(2,1)S(1)}, bf16[10,1,256]{2,1,0:T(2,128)(2,1)S(1)}, u32[]{:S(2)}, u32[]{:S(2)}) collective-permute-start(bf16[10,1,256]{2,1,0:T(2,128)(2,1)S(1)} %get-tuple-element.19), channel_id=1, source_target_pairs={{0,1},{1,2},{2,3},{3,4},{4,5},{5,6},{6,7},{8,9},{9,10},{10,11},{11... | collective-permute-start | bytes 15368 | tf_op jit(solution)/shard_map/ppermute | solution.py:15
  26.3 5.9 collective-permute-start.3
  32.5 1.7 copy-start.1
  36.8 1.3 copy-start.4
  38.1 258.4 %copy-start.3 = (f32[2,512]{1,0:T(2,128)S(1)}, f32[2,512]{1,0:T(2,128)}, u32[]{:S(2)}) copy-start(f32[2,512]{1,0:T(2,128)} %param.7) | copy-start | bytes 12292
  40.9 636.6 %all-gather.3.cloned.1.call-start = ((), (), s32[]{:S(2)}) async-start(), calls=%async_computation | async-start | bytes 1052672 | tf_op jit(solution)/shard_map/all_gather | solution.py:61
  685.0 11.6 %collective-permute-start.5 = (bf16[1,128,512]{2,1,0:T(8,128)(2,1)}, bf16[1,128,512]{2,1,0:T(8,128)(2,1)S(1)}, u32[]{:S(2)}, u32[]{:S(2)}) collective-permute-start(bf16[1,128,512]{2,1,0:T(8,128)(2,1)} %get-tuple-element.17), channel_id=1, source_target_pairs={{8,0},{16,8},{24,16},{32,24},{40,32},{48,40},{56,48},{64,56},{72,6... | collective-permute-start | bytes 393224 | tf_op jit(solution)/shard_map/ppermute | solution.py:18
  690.3 10.9 %collective-permute-start.4 = (bf16[1,128,512]{2,1,0:T(8,128)(2,1)}, bf16[1,128,512]{2,1,0:T(8,128)(2,1)}, u32[]{:S(2)}, u32[]{:S(2)}) collective-permute-start(bf16[1,128,512]{2,1,0:T(8,128)(2,1)} %get-tuple-element.16), channel_id=1, source_target_pairs={{0,8},{8,16},{16,24},{24,32},{32,40},{40,48},{48,56},{56,64},{64,7... | collective-permute-start | bytes 393224 | tf_op jit(solution)/shard_map/ppermute | solution.py:15
  701.9 8.1 %collective-permute-start.7 = (bf16[10,1,512]{2,1,0:T(2,128)(2,1)S(1)}, bf16[10,1,512]{2,1,0:T(2,128)(2,1)S(1)}, u32[]{:S(2)}, u32[]{:S(2)}) collective-permute-start(bf16[10,1,512]{2,1,0:T(2,128)(2,1)S(1)} %get-tuple-element.12), channel_id=1, source_target_pairs={{1,0},{2,1},{3,2},{4,3},{5,4},{6,5},{7,6},{9,8},{10,9},{11,10},{12... | collective-permute-start | bytes 30728 | tf_op jit(solution)/shard_map/ppermute | solution.py:18
  705.3 4.8 collective-permute-start.6
  713.0 1.7 copy-start.2
Sparse Core Ops, SparseCore 0:
  41.0 255.4 all-reduce.2
  299.0 378.4 all-gather.2
where the time goes:
time: 726 us; the launch traced here: 725 us
  waiting for transfers between devices  644 us (89%)
  starting transfers between devices  32.2 us (4%)
  local copies, waits for them, and re-layouts  15 us (2%)
  between operations  14.4 us (2%)
  matrix products  13.3 us (2%)
    all_gather x1, waiting for transfers between devices, on_device(): error_full = lax.all_gather(error_own, ('rows', 'cols'), axis=0, tiled=True)  380 us
    unnamed x3, waiting for transfers between devices  256 us
    ppermute x4, starting transfers between devices, padded_2(): lax.ppermute(lax.slice_in_dim(block, 0, width, axis=dim), axis, backward)  16.8 us
    ppermute x4, starting transfers between devices, padded_2(): lax.ppermute(lax.slice_in_dim(block, block.shape[dim] - width, None, axis...  15.3 us
  transfers between devices with their start and end apart: 10, of which 5 were waited for; matrix products, arithmetic and copies ran while one was open for 1% of the time, Pallas kernels for 0%

commit v1 on v0

--- a/solution.py
+++ b/solution.py
@@ -58,7 +58,12 @@
         / pixel_total
     )
     error_own = gram_own - target_gram
-    error_full = lax.all_gather(error_own, ("rows", "cols"), axis=0, tiled=True)
+    error_full = jnp.concatenate(
+        lax.all_to_all(
+            jnp.stack([error_own] * lax.axis_size(("rows", "cols"))), ("rows", "cols"), 0, 0
+        ),
+        axis=0,
+    )
     symmetric = (error_full + error_full.T).astype(jnp.bfloat16)
     upstream = jnp.dot(features, symmetric, preferred_element_type=jnp.float32) / math.sqrt(
         out_width

time: 726 us -> 386 us (0.53)
  waiting for transfers between devices: 644 us -> 263 us
  blocking collectives: 0 us -> 43.3 us
    all_gather x1 -> x0, waiting for transfers between devices: 380 us -> none  [on_device(): error_full = lax.all_gather(error_own, ('rows', 'cols'), axis=0, tiled=True)]
    all_to_all x0 -> x1, blocking collectives: none -> 43.3 us  [on_device(): lax.all_to_all(jnp.stack([error_own] * lax.axis_size(('rows', 'cols'))),...]
    unnamed x3 -> x2, waiting for transfers between devices: 256 us -> 256 us
  transfers between devices with their start and end apart: 10 -> 9, of which waited for: 5 -> 4; matrix products, arithmetic and copies ran while one was open for 1% -> 2% of each run, Pallas kernels for 0% -> 0%
where the time goes in v1:
time: 386 us
  waiting for transfers between devices  263 us (68%)
  blocking collectives  43.3 us (11%)
  starting transfers between devices  31 us (8%)
  between operations  14.4 us (4%)
  local copies, waits for them, and re-layouts  14 us (4%)
  matrix products  13.3 us (3%)
  other arithmetic  6.28 us (2%)
    unnamed x2, waiting for transfers between devices  256 us
    all_to_all x1, blocking collectives, on_device(): lax.all_to_all(jnp.stack([error_own] * lax.axis_size(('rows', 'cols'))),...  43.3 us
    ppermute x4, starting transfers between devices, padded_2(): lax.ppermute(lax.slice_in_dim(block, 0, width, axis=dim), axis, backward)  16.6 us
    ppermute x4, starting transfers between devices, padded_2(): lax.ppermute(lax.slice_in_dim(block, block.shape[dim] - width, None, axis...  14.3 us
    unnamed x22, local copies, waits for them, and re-layouts  8.54 us
  transfers between devices with their start and end apart: 9, of which 4 were waited for; matrix products, arithmetic and copies ran while one was open for 2% of the time, Pallas kernels for 0%

profile of v1, /device:TPU:33, one launch (start us, length us, event | category | flops | bytes accessed | tf_op | source)
XLA Modules:
  0.0 385.6 jit_solution(4199634923770314276)
XLA Ops:
  8.2 3.1 collective-permute-start
  11.3 6.4 %collective-permute-start.1 = (bf16[1,128,256]{2,1,0:T(8,128)(2,1)S(1)}, bf16[1,128,256]{2,1,0:T(8,128)(2,1)S(1)}, u32[]{:S(2)}, u32[]{:S(2)}) collective-permute-start(bf16[1,128,256]{2,1,0:T(8,128)(2,1)S(1)} %get-tuple-element.20), channel_id=1, source_target_pairs={{8,0},{16,8},{24,16},{32,24},{40,32},{48,40},{56,48},{64,56},{72,6... | collective-permute-start | bytes 196616 | tf_op jit(solution)/shard_map/ppermute | solution.py:18
  19.0 6.6 %collective-permute-start.2 = (bf16[10,1,256]{2,1,0:T(2,128)(2,1)S(1)}, bf16[10,1,256]{2,1,0:T(2,128)(2,1)S(1)}, u32[]{:S(2)}, u32[]{:S(2)}) collective-permute-start(bf16[10,1,256]{2,1,0:T(2,128)(2,1)S(1)} %get-tuple-element.19), channel_id=1, source_target_pairs={{0,1},{1,2},{2,3},{3,4},{4,5},{5,6},{6,7},{8,9},{9,10},{10,11},{11... | collective-permute-start | bytes 15368 | tf_op jit(solution)/shard_map/ppermute | solution.py:15
  26.3 1.9 collective-permute-start.3
  28.4 3.8 collective-permute-done.3
  33.0 1.2 copy-done.1
  34.2 2.6 fusion.45
  36.8 1.3 copy-done.4
  38.1 2.8 fusion.30
  40.9 255.6 %all-reduce.3.cloned.1.call-done = f32[512,512]{1,0:T(8,128)} async-done(((f32[512,512]{1,0:T(8,128)}), f32[512,512]{1,0:T(8,128)}) %all-reduce.3.cloned.1.call-update) | async-done | bytes 1048592
  296.5 1.3 fusion.40
  298.1 43.3 %all_to_all.5 = f32[256,2,512]{2,1,0:T(2,128)S(1)} all-to-all(f32[256,2,512]{2,1,0:T(2,128)S(1)} %stack.2), channel_id=1, replica_groups=mesh['rows'=32,'cols'=8] {'rows','cols'}, dimensions={0} | all-to-all | bytes 2097152 | tf_op jit(solution)/shard_map/all_to_all | solution.py:62
  342.5 4.5 %fusion.14 = bf16[1024,512]{1,0:T(8,128)(2,1)S(1)} fusion(f32[1024,512]{1,0:T(8,128)} %copy-done.4, f32[512]{0:T(512)S(1)} %convert_element_type.15, f32[512,512]{1,0:T(8,128)S(1)} %reshape.40, f32[512,512]{0,1:T(8,128)S(1)} %copy.9), kind=kOutput, calls=%fused_computation.17 | convolution fusion | flops 553648128 | bytes 5244928 | tf_op jit(solution)/shard_map/dot_general | solution.py:68
  347.7 3.2 collective-permute-start.5
  351.0 2.1 collective-permute-start.4
  353.0 2.8 copy.10
  355.9 1.6 rev.3
  357.5 3.7 collective-permute-done.4
  362.0 5.1 %collective-permute-start.7 = (bf16[10,1,512]{2,1,0:T(2,128)(2,1)S(1)}, bf16[10,1,512]{2,1,0:T(2,128)(2,1)S(1)}, u32[]{:S(2)}, u32[]{:S(2)}) collective-permute-start(bf16[10,1,512]{2,1,0:T(2,128)(2,1)S(1)} %get-tuple-element.12), channel_id=1, source_target_pairs={{1,0},{2,1},{3,2},{4,3},{5,4},{6,5},{7,6},{9,8},{10,9},{11,10},{12... | collective-permute-start | bytes 30728 | tf_op jit(solution)/shard_map/ppermute | solution.py:18
  367.1 2.6 collective-permute-start.6
  369.6 1.1 pad_maximum_fusion.1
  370.8 1.6 pad_maximum_fusion
  373.9 1.5 copy-done.2
  375.4 3.4 convolution_convert_fusion
  (45 shorter events, 8.2 us)
Async XLA Ops:
  7.2 21.2 %copy-start = (bf16[8,128,256]{2,1,0:T(8,128)(2,1)S(1)}, bf16[8,128,256]{2,1,0:T(8,128)(2,1)}, u32[]{:S(2)}) copy-start(bf16[8,128,256]{2,1,0:T(8,128)(2,1)} %param.4) | copy-start | bytes 1572868
  7.2 289.4 %all-reduce.3.cloned.1.call-start = ((), (), s32[]{:S(2)}) async-start(), calls=%async_computation.1 | async-start | bytes 2097152
  8.2 9.5 %collective-permute-start = (bf16[1,128,256]{2,1,0:T(8,128)(2,1)S(1)}, bf16[1,128,256]{2,1,0:T(8,128)(2,1)S(1)}, u32[]{:S(2)}, u32[]{:S(2)}) collective-permute-start(bf16[1,128,256]{2,1,0:T(8,128)(2,1)S(1)} %get-tuple-element.21), channel_id=1, source_target_pairs={{0,8},{8,16},{16,24},{24,32},{32,40},{40,48},{48,56},{56,64},{64,7... | collective-permute-start | bytes 196616 | tf_op jit(solution)/shard_map/ppermute | solution.py:15
  11.3 7.7 %collective-permute-start.1 = (bf16[1,128,256]{2,1,0:T(8,128)(2,1)S(1)}, bf16[1,128,256]{2,1,0:T(8,128)(2,1)S(1)}, u32[]{:S(2)}, u32[]{:S(2)}) collective-permute-start(bf16[1,128,256]{2,1,0:T(8,128)(2,1)S(1)} %get-tuple-element.20), channel_id=1, source_target_pairs={{8,0},{16,8},{24,16},{32,24},{40,32},{48,40},{56,48},{64,56},{72,6... | collective-permute-start | bytes 196616 | tf_op jit(solution)/shard_map/ppermute | solution.py:18
  19.0 9.2 %collective-permute-start.2 = (bf16[10,1,256]{2,1,0:T(2,128)(2,1)S(1)}, bf16[10,1,256]{2,1,0:T(2,128)(2,1)S(1)}, u32[]{:S(2)}, u32[]{:S(2)}) collective-permute-start(bf16[10,1,256]{2,1,0:T(2,128)(2,1)S(1)} %get-tuple-element.19), channel_id=1, source_target_pairs={{0,1},{1,2},{2,3},{3,4},{4,5},{5,6},{6,7},{8,9},{9,10},{10,11},{11... | collective-permute-start | bytes 15368 | tf_op jit(solution)/shard_map/ppermute | solution.py:15
  26.3 5.9 %collective-permute-start.3 = (bf16[10,1,256]{2,1,0:T(2,128)(2,1)S(1)}, bf16[10,1,256]{2,1,0:T(2,128)(2,1)S(1)}, u32[]{:S(2)}, u32[]{:S(2)}) collective-permute-start(bf16[10,1,256]{2,1,0:T(2,128)(2,1)S(1)} %get-tuple-element.18), channel_id=1, source_target_pairs={{1,0},{2,1},{3,2},{4,3},{5,4},{6,5},{7,6},{9,8},{10,9},{11,10},{12... | collective-permute-start | bytes 15368 | tf_op jit(solution)/shard_map/ppermute | solution.py:18
  32.5 1.7 copy-start.1
  36.8 1.3 copy-start.4
  38.1 258.4 %copy-start.3 = (f32[2,512]{1,0:T(2,128)S(1)}, f32[2,512]{1,0:T(2,128)}, u32[]{:S(2)}) copy-start(f32[2,512]{1,0:T(2,128)} %param.7) | copy-start | bytes 12292
  347.7 9.7 %collective-permute-start.5 = (bf16[1,128,512]{2,1,0:T(8,128)(2,1)}, bf16[1,128,512]{2,1,0:T(8,128)(2,1)S(1)}, u32[]{:S(2)}, u32[]{:S(2)}) collective-permute-start(bf16[1,128,512]{2,1,0:T(8,128)(2,1)} %get-tuple-element.17), channel_id=1, source_target_pairs={{8,0},{16,8},{24,16},{32,24},{40,32},{48,40},{56,48},{64,56},{72,6... | collective-permute-start | bytes 393224 | tf_op jit(solution)/shard_map/ppermute | solution.py:18
  351.0 10.2 %collective-permute-start.4 = (bf16[1,128,512]{2,1,0:T(8,128)(2,1)}, bf16[1,128,512]{2,1,0:T(8,128)(2,1)}, u32[]{:S(2)}, u32[]{:S(2)}) collective-permute-start(bf16[1,128,512]{2,1,0:T(8,128)(2,1)} %get-tuple-element.16), channel_id=1, source_target_pairs={{0,8},{8,16},{16,24},{24,32},{32,40},{40,48},{48,56},{56,64},{64,7... | collective-permute-start | bytes 393224 | tf_op jit(solution)/shard_map/ppermute | solution.py:15
  362.0 8.8 %collective-permute-start.7 = (bf16[10,1,512]{2,1,0:T(2,128)(2,1)S(1)}, bf16[10,1,512]{2,1,0:T(2,128)(2,1)S(1)}, u32[]{:S(2)}, u32[]{:S(2)}) collective-permute-start(bf16[10,1,512]{2,1,0:T(2,128)(2,1)S(1)} %get-tuple-element.12), channel_id=1, source_target_pairs={{1,0},{2,1},{3,2},{4,3},{5,4},{6,5},{7,6},{9,8},{10,9},{11,10},{12... | collective-permute-start | bytes 30728 | tf_op jit(solution)/shard_map/ppermute | solution.py:18
  367.1 3.7 collective-permute-start.6
  373.7 1.7 copy-start.2
Sparse Core Ops, SparseCore 0:
  41.0 255.4 all-reduce.2
